TPU v7x, 256 devices: a whole 4x4x8 slice. The times are simulated.
256 devices in a mesh: view: 8 (over y_lo, x), tile: 32 (over y_hi, z, core).
Axes of the slice: x: 4, y: 4 (y_hi: 2, y_lo: 2; y = y_hi * 2 + y_lo), z: 8, core: 2. Of those that a mesh axis runs over, the one named last changes fastest.
Arguments:
- estimate: float32 [1024, 64, 256], P('tile'), may hold values from 0.5 to 2
- measured: bfloat16 [8, 1024, 64, 256], P('view', 'tile'), may hold values from 0.5 to 2
- blur_profile: float32 [8, 256], P('view'), may hold values from 0.1 to 1
- view_offset: int32 [8], P('view'), may hold values from -6 to 6, as said below
- tile_shift: int32 [8], P('view'), may hold values from 0 to 31
Outputs:
- updated: float32 [1024, 64, 256], P('tile')
Inputs may be any that keep to these rules, and one draw needn't show every extreme that they name: `view_offset`: some view has offset 6 and some other view has offset -6.
All inputs are finite; a program needn't handle non-finite values.
Results may differ from a plain program's by a relative error of at most 0.0016.
Values may be sent and summed in bfloat16 or wider, within the bound.
No kernel may reach another device: no remote copies, remote signals or barrier semaphores. Data moves between devices by JAX's collectives and lax.ppermute only.
A program may use at most 64 MiB of HBM per device.

v0:
```python
import math
import jax
import jax.numpy as jnp
from jax import lax
from jax.sharding import PartitionSpec as P

H = 6
profile_sigma = 48.0


def with_halo(cells, sides, width):
    for axis, dim in sides:
        count = lax.axis_size(axis)
        head = lax.slice_in_dim(cells, 0, width, axis=dim)
        tail = lax.slice_in_dim(cells, cells.shape[dim] - width, cells.shape[dim], axis=dim)
        cells = jnp.concatenate(
            [
                lax.ppermute(tail, axis, [(i, (i + 1) % count) for i in range(count)]),
                cells,
                lax.ppermute(head, axis, [((i + 1) % count, i) for i in range(count)]),
            ],
            axis=dim,
        )
    return cells


def from_behind(block, axis, distance):
    devices = range(lax.axis_size(axis))
    route = [((i - distance) % len(devices), i) for i in devices]
    return lax.ppermute(block, axis, route)


def make_kernel(profile):
    length = profile.shape[0]
    column = jnp.arange(length)
    distance = jnp.minimum(column, length - column).astype(jnp.float32)
    weights = profile * jnp.exp(-distance * distance / (2.0 * profile_sigma * profile_sigma))
    return weights / jnp.sum(weights)


def matmul_high(left, right):
    return jnp.dot(left, right, precision=lax.Precision.HIGHEST, preferred_element_type=jnp.float32)


def body(estimate, measured, blur_profile, view_offset, tile_shift):
    view_count = lax.axis_size("view")
    view_index = lax.axis_index("view")
    blend_weight = (view_index + 1).astype(jnp.float32) / (view_count + 1)
    kernel = make_kernel(blur_profile[0])
    offset = view_offset[0]
    tile_move = tile_shift[0]
    length = estimate.shape[2]
    halo_width = H + 1
    bit_count = (lax.axis_size("tile") - 1).bit_length()
    column = jnp.arange(length)
    phase = column[:, None] * column[None, :] % length
    angle = phase.astype(jnp.float32) * (2.0 * math.pi / length)
    cosine = jnp.cos(angle)
    sine_table = jnp.sin(angle)
    spec_real = matmul_high(kernel, cosine)
    spec_imag = -matmul_high(kernel, sine_table)

    def blur_along(volume, adjoint):
        imag_kernel = -spec_imag if adjoint else spec_imag
        real_part = matmul_high(volume, cosine)
        imag_part = -matmul_high(volume, sine_table)
        out_real = real_part * spec_real - imag_part * imag_kernel
        out_imag = real_part * imag_kernel + imag_part * spec_real
        return (matmul_high(out_real, cosine) - matmul_high(out_imag, sine_table)) / length

    relocated = estimate
    for level in range(bit_count):
        stride = 1 << level
        arrived = from_behind(relocated.astype(jnp.bfloat16), "tile", -stride).astype(
            relocated.dtype
        )
        relocated = jnp.where(tile_move // stride % 2 == 1, arrived, relocated)
    padded = with_halo(relocated, (("tile", 0),), halo_width)
    rows = relocated.shape[0]
    first = lax.dynamic_slice_in_dim(padded, halo_width + offset, rows, 0)
    second = lax.dynamic_slice_in_dim(padded, halo_width + offset + 1, rows, 0)
    forward = blur_along(blend_weight * first + (1.0 - blend_weight) * second, False)
    ratios = measured[0].astype(jnp.float32) / forward
    volume = blur_along(ratios, True)
    padded = with_halo(volume, (("tile", 0),), halo_width)
    rows = volume.shape[0]
    first = lax.dynamic_slice_in_dim(padded, halo_width - offset, rows, 0)
    second = lax.dynamic_slice_in_dim(padded, halo_width - offset - 1, rows, 0)
    correction = blend_weight * first + (1.0 - blend_weight) * second
    for level in range(bit_count):
        stride = 1 << level
        arrived = from_behind(correction, "tile", stride)
        correction = jnp.where(tile_move // stride % 2 == 1, arrived, correction)
    log_terms = jnp.log(correction)
    summed = lax.psum(log_terms, "view")
    return estimate * jnp.exp(summed)


def solution(mesh):
    placed = (
        P("tile", None, None),
        P("view", "tile", None, None),
        P("view", None),
        P("view"),
        P("view"),
    )
    return jax.shard_map(
        body, mesh=mesh, in_specs=placed, out_specs=P("tile", None, None), check_vma=False
    )
```

profile of v0, /device:TPU:32, one launch (start us, length us, event | category | flops | bytes accessed | tf_op | source)
XLA Modules:
  0.0 745.7 jit_solution(8670990774222465612)
XLA Ops:
  10.1 12.0 %collective-permute-done = bf16[32,64,256]{2,1,0:T(8,128)(2,1)S(1)} collective-permute-done((bf16[32,64,256]{2,1,0:T(8,128)(2,1)}, bf16[32,64,256]{2,1,0:T(8,128)(2,1)S(1)}, u32[]{:S(2)}, u32[]{:S(2)}) %collective-permute-start) | collective-permute-done | bytes 1048608 | tf_op jit(solution)/shard_map/ppermute | solution.py:30
  23.4 8.0 %collective-permute-start.1 = (bf16[32,64,256]{2,1,0:T(8,128)(2,1)}, bf16[32,64,256]{2,1,0:T(8,128)(2,1)}, u32[]{:S(2)}, u32[]{:S(2)}) collective-permute-start(bf16[32,64,256]{2,1,0:T(8,128)(2,1)} %fusion.22), channel_id=1, source_target_pairs={{2,0},{3,1},{4,2},{5,3},{6,4},{7,5},{8,6},{9,7},{10,8},{11,9},{12,... | collective-permute-start | bytes 3145736 | tf_op jit(solution)/shard_map/ppermute | solution.py:30
  31.4 17.2 %collective-permute-done.1 = bf16[32,64,256]{2,1,0:T(8,128)(2,1)} collective-permute-done((bf16[32,64,256]{2,1,0:T(8,128)(2,1)}, bf16[32,64,256]{2,1,0:T(8,128)(2,1)}, u32[]{:S(2)}, u32[]{:S(2)}) %collective-permute-start.1) | collective-permute-done | bytes 1048608 | tf_op jit(solution)/shard_map/ppermute | solution.py:30
  48.6 3.5 fusion.112
  52.1 9.3 %collective-permute-start.2 = (bf16[32,64,256]{2,1,0:T(8,128)(2,1)}, bf16[32,64,256]{2,1,0:T(8,128)(2,1)S(1)}, u32[]{:S(2)}, u32[]{:S(2)}) collective-permute-start(bf16[32,64,256]{2,1,0:T(8,128)(2,1)} %get-tuple-element.5), channel_id=1, source_target_pairs={{4,0},{5,1},{6,2},{7,3},{8,4},{9,5},{10,6},{11,7},{12,8},{13,9},{1... | collective-permute-start | bytes 3145736 | tf_op jit(solution)/shard_map/ppermute | solution.py:30
  61.4 41.3 %collective-permute-done.2 = bf16[32,64,256]{2,1,0:T(8,128)(2,1)S(1)} collective-permute-done((bf16[32,64,256]{2,1,0:T(8,128)(2,1)}, bf16[32,64,256]{2,1,0:T(8,128)(2,1)S(1)}, u32[]{:S(2)}, u32[]{:S(2)}) %collective-permute-start.2) | collective-permute-done | bytes 1048608 | tf_op jit(solution)/shard_map/ppermute | solution.py:30
  104.1 9.1 %collective-permute-start.3 = (bf16[32,64,256]{2,1,0:T(8,128)(2,1)}, bf16[32,64,256]{2,1,0:T(8,128)(2,1)}, u32[]{:S(2)}, u32[]{:S(2)}) collective-permute-start(bf16[32,64,256]{2,1,0:T(8,128)(2,1)} %fusion.23), channel_id=1, source_target_pairs={{8,0},{9,1},{10,2},{11,3},{12,4},{13,5},{14,6},{15,7},{16,8},{17,9... | collective-permute-start | bytes 3145736 | tf_op jit(solution)/shard_map/ppermute | solution.py:30
  113.2 45.5 %collective-permute-done.3 = bf16[32,64,256]{2,1,0:T(8,128)(2,1)} collective-permute-done((bf16[32,64,256]{2,1,0:T(8,128)(2,1)}, bf16[32,64,256]{2,1,0:T(8,128)(2,1)}, u32[]{:S(2)}, u32[]{:S(2)}) %collective-permute-start.3) | collective-permute-done | bytes 1048608 | tf_op jit(solution)/shard_map/ppermute | solution.py:30
  163.9 23.7 %collective-permute-done.4 = bf16[32,64,256]{2,1,0:T(8,128)(2,1)} collective-permute-done((bf16[32,64,256]{2,1,0:T(8,128)(2,1)}, bf16[32,64,256]{2,1,0:T(8,128)(2,1)}, u32[]{:S(2)}, u32[]{:S(2)}) %collective-permute-start.4) | collective-permute-done | bytes 1048608 | tf_op jit(solution)/shard_map/ppermute | solution.py:30
  202.0 2.9 fusion.35
  205.0 2.9 fusion.36
  207.9 3.0 fusion.8
  210.9 3.3 convert_divide_fusion
  219.9 3.0 fusion
  222.9 3.2 subtract_multiply_fusion
  230.4 6.4 collective-permute-done.7
  239.6 25.3 %collective-permute-done.9 = f32[32,64,256]{2,1,0:T(8,128)S(1)} collective-permute-done((f32[32,64,256]{2,1,0:T(8,128)S(1)}, f32[32,64,256]{2,1,0:T(8,128)S(1)}, u32[]{:S(2)}, u32[]{:S(2)}) %collective-permute-start.9) | collective-permute-done | bytes 2097184 | tf_op jit(solution)/shard_map/ppermute | solution.py:30
  266.0 45.6 %collective-permute-done.10 = f32[32,64,256]{2,1,0:T(8,128)S(1)} collective-permute-done((f32[32,64,256]{2,1,0:T(8,128)S(1)}, f32[32,64,256]{2,1,0:T(8,128)S(1)}, u32[]{:S(2)}, u32[]{:S(2)}) %collective-permute-start.10) | collective-permute-done | bytes 2097184 | tf_op jit(solution)/shard_map/ppermute | solution.py:30
  311.9 5.0 collective-permute-start.11
  317.0 94.2 %collective-permute-done.11 = f32[32,64,256]{2,1,0:T(8,128)S(1)} collective-permute-done((f32[32,64,256]{2,1,0:T(8,128)S(1)}, f32[32,64,256]{2,1,0:T(8,128)S(1)}, u32[]{:S(2)}, u32[]{:S(2)}) %collective-permute-start.11) | collective-permute-done | bytes 2097184 | tf_op jit(solution)/shard_map/ppermute | solution.py:30
  411.7 98.0 %collective-permute-done.12 = f32[32,64,256]{2,1,0:T(8,128)S(1)} collective-permute-done((f32[32,64,256]{2,1,0:T(8,128)S(1)}, f32[32,64,256]{2,1,0:T(8,128)S(1)}, u32[]{:S(2)}, u32[]{:S(2)}) %collective-permute-start.12) | collective-permute-done | bytes 2097184 | tf_op jit(solution)/shard_map/ppermute | solution.py:30
  511.3 45.6 %collective-permute-done.13 = f32[32,64,256]{2,1,0:T(8,128)S(1)} collective-permute-done((f32[32,64,256]{2,1,0:T(8,128)S(1)}, f32[32,64,256]{2,1,0:T(8,128)S(1)}, u32[]{:S(2)}, u32[]{:S(2)}) %collective-permute-start.13) | collective-permute-done | bytes 2097184 | tf_op jit(solution)/shard_map/ppermute | solution.py:30
  558.6 176.6 %all-reduce.2.cloned.1.call-done = f32[32,64,256]{2,1,0:T(8,128)} async-done(((f32[32,64,256]{2,1,0:T(8,128)}), f32[32,64,256]{2,1,0:T(8,128)}) %all-reduce.2.cloned.1.call-update) | async-done | bytes 2097168 | tf_op jit(solution)/shard_map/psum | solution.py:95
  735.2 3.4 exponential_multiply_fusion
  (47 shorter events, 42.4 us)
Async XLA Ops:
  6.5 15.5 %copy-start = (f32[32,64,256]{2,1,0:T(8,128)S(1)}, f32[32,64,256]{2,1,0:T(8,128)}, u32[]{:S(2)}) copy-start(f32[32,64,256]{2,1,0:T(8,128)} %param.5) | copy-start | bytes 6291460
  6.5 728.7 %all-reduce.2.cloned.1.call-start = ((), (), s32[]{:S(2)}) async-start(), calls=%async_computation | async-start | bytes 4194304 | tf_op jit(solution)/shard_map/psum | solution.py:95
  9.4 12.6 %collective-permute-start = (bf16[32,64,256]{2,1,0:T(8,128)(2,1)}, bf16[32,64,256]{2,1,0:T(8,128)(2,1)S(1)}, u32[]{:S(2)}, u32[]{:S(2)}) collective-permute-start(bf16[32,64,256]{2,1,0:T(8,128)(2,1)} %convert_element_type.66), channel_id=1, source_target_pairs={{1,0},{2,1},{3,2},{4,3},{5,4},{6,5},{7,6},{8,7},{9,8},{10,9},{11,1... | collective-permute-start | bytes 3145736 | tf_op jit(solution)/shard_map/ppermute | solution.py:30
  23.4 25.3 %collective-permute-start.1 = (bf16[32,64,256]{2,1,0:T(8,128)(2,1)}, bf16[32,64,256]{2,1,0:T(8,128)(2,1)}, u32[]{:S(2)}, u32[]{:S(2)}) collective-permute-start(bf16[32,64,256]{2,1,0:T(8,128)(2,1)} %fusion.22), channel_id=1, source_target_pairs={{2,0},{3,1},{4,2},{5,3},{6,4},{7,5},{8,6},{9,7},{10,8},{11,9},{12,... | collective-permute-start | bytes 3145736 | tf_op jit(solution)/shard_map/ppermute | solution.py:30
  52.1 50.7 %collective-permute-start.2 = (bf16[32,64,256]{2,1,0:T(8,128)(2,1)}, bf16[32,64,256]{2,1,0:T(8,128)(2,1)S(1)}, u32[]{:S(2)}, u32[]{:S(2)}) collective-permute-start(bf16[32,64,256]{2,1,0:T(8,128)(2,1)} %get-tuple-element.5), channel_id=1, source_target_pairs={{4,0},{5,1},{6,2},{7,3},{8,4},{9,5},{10,6},{11,7},{12,8},{13,9},{1... | collective-permute-start | bytes 3145736 | tf_op jit(solution)/shard_map/ppermute | solution.py:30
  104.1 54.6 %collective-permute-start.3 = (bf16[32,64,256]{2,1,0:T(8,128)(2,1)}, bf16[32,64,256]{2,1,0:T(8,128)(2,1)}, u32[]{:S(2)}, u32[]{:S(2)}) collective-permute-start(bf16[32,64,256]{2,1,0:T(8,128)(2,1)} %fusion.23), channel_id=1, source_target_pairs={{8,0},{9,1},{10,2},{11,3},{12,4},{13,5},{14,6},{15,7},{16,8},{17,9... | collective-permute-start | bytes 3145736 | tf_op jit(solution)/shard_map/ppermute | solution.py:30
  113.2 50.1 %copy-start.3 = (f32[1,256]{1,0:T(1,128)S(1)}, f32[1,256]{1,0:T(1,128)}, u32[]{:S(2)}) copy-start(f32[1,256]{1,0:T(1,128)} %param.7) | copy-start | bytes 3076
  161.4 26.2 %collective-permute-start.4 = (bf16[32,64,256]{2,1,0:T(8,128)(2,1)}, bf16[32,64,256]{2,1,0:T(8,128)(2,1)}, u32[]{:S(2)}, u32[]{:S(2)}) collective-permute-start(bf16[32,64,256]{2,1,0:T(8,128)(2,1)} %fusion.34), channel_id=1, source_target_pairs={{16,0},{17,1},{18,2},{19,3},{20,4},{21,5},{22,6},{23,7},{24,8},{25... | collective-permute-start | bytes 3145736 | tf_op jit(solution)/shard_map/ppermute | solution.py:30
  189.8 1.3 copy-start.2
  191.9 8.1 %collective-permute-start.5 = (f32[7,64,256]{2,1,0:T(8,128)}, f32[7,64,256]{2,1,0:T(8,128)S(1)}, u32[]{:S(2)}, u32[]{:S(2)}) collective-permute-start(f32[7,64,256]{2,1,0:T(8,128)} %get-tuple-element.9), channel_id=1, source_target_pairs={{0,1},{1,2},{2,3},{3,4},{4,5},{5,6},{6,7},{7,8},{8,9},{9,10},{10,1... | collective-permute-start | bytes 1376264 | tf_op jit(solution)/shard_map/ppermute | solution.py:18
  191.9 8.2 %collective-permute-start.6 = (f32[7,64,256]{2,1,0:T(8,128)S(1)}, f32[7,64,256]{2,1,0:T(8,128)S(1)}, u32[]{:S(2)}, u32[]{:S(2)}) collective-permute-start(f32[7,64,256]{2,1,0:T(8,128)S(1)} %get-tuple-element.10), channel_id=1, source_target_pairs={{1,0},{2,1},{3,2},{4,3},{5,4},{6,5},{7,6},{8,7},{9,8},{10,9},{11,1... | collective-permute-start | bytes 1376264 | tf_op jit(solution)/shard_map/ppermute | solution.py:20
  207.9 3.0 copy-start.4
  226.0 1.3 copy-start.1
  228.2 8.6 %collective-permute-start.7 = (f32[7,64,256]{2,1,0:T(8,128)}, f32[7,64,256]{2,1,0:T(8,128)S(1)}, u32[]{:S(2)}, u32[]{:S(2)}) collective-permute-start(f32[7,64,256]{2,1,0:T(8,128)} %get-tuple-element.7), channel_id=1, source_target_pairs={{0,1},{1,2},{2,3},{3,4},{4,5},{5,6},{6,7},{7,8},{8,9},{9,10},{10,1... | collective-permute-start | bytes 1376264 | tf_op jit(solution)/shard_map/ppermute | solution.py:18
  229.2 7.6 %collective-permute-start.8 = (f32[7,64,256]{2,1,0:T(8,128)S(1)}, f32[7,64,256]{2,1,0:T(8,128)S(1)}, u32[]{:S(2)}, u32[]{:S(2)}) collective-permute-start(f32[7,64,256]{2,1,0:T(8,128)S(1)} %get-tuple-element.8), channel_id=1, source_target_pairs={{1,0},{2,1},{3,2},{4,3},{5,4},{6,5},{7,6},{8,7},{9,8},{10,9},{11,1... | collective-permute-start | bytes 1376264 | tf_op jit(solution)/shard_map/ppermute | solution.py:20
  239.2 25.6 %collective-permute-start.9 = (f32[32,64,256]{2,1,0:T(8,128)S(1)}, f32[32,64,256]{2,1,0:T(8,128)S(1)}, u32[]{:S(2)}, u32[]{:S(2)}) collective-permute-start(f32[32,64,256]{2,1,0:T(8,128)S(1)} %multiply_add_fusion), channel_id=1, source_target_pairs={{31,0},{0,1},{1,2},{2,3},{3,4},{4,5},{5,6},{6,7},{7,8},{8,9},{9,10... | collective-permute-start | bytes 6291464 | tf_op jit(solution)/shard_map/ppermute | solution.py:30
  265.6 46.0 %collective-permute-start.10 = (f32[32,64,256]{2,1,0:T(8,128)S(1)}, f32[32,64,256]{2,1,0:T(8,128)S(1)}, u32[]{:S(2)}, u32[]{:S(2)}) collective-permute-start(f32[32,64,256]{2,1,0:T(8,128)S(1)} %broadcast_select_fusion), channel_id=1, source_target_pairs={{30,0},{31,1},{0,2},{1,3},{2,4},{3,5},{4,6},{5,7},{6,8},{7,9},{8,1... | collective-permute-start | bytes 6291464 | tf_op jit(solution)/shard_map/ppermute | solution.py:30
  311.9 99.3 %collective-permute-start.11 = (f32[32,64,256]{2,1,0:T(8,128)S(1)}, f32[32,64,256]{2,1,0:T(8,128)S(1)}, u32[]{:S(2)}, u32[]{:S(2)}) collective-permute-start(f32[32,64,256]{2,1,0:T(8,128)S(1)} %broadcast_select_fusion.1), channel_id=1, source_target_pairs={{28,0},{29,1},{30,2},{31,3},{0,4},{1,5},{2,6},{3,7},{4,8},{5,9},{6... | collective-permute-start | bytes 6291464 | tf_op jit(solution)/shard_map/ppermute | solution.py:30
  411.6 98.1 %collective-permute-start.12 = (f32[32,64,256]{2,1,0:T(8,128)S(1)}, f32[32,64,256]{2,1,0:T(8,128)S(1)}, u32[]{:S(2)}, u32[]{:S(2)}) collective-permute-start(f32[32,64,256]{2,1,0:T(8,128)S(1)} %broadcast_select_fusion.2), channel_id=1, source_target_pairs={{24,0},{25,1},{26,2},{27,3},{28,4},{29,5},{30,6},{31,7},{0,8},{1,9... | collective-permute-start | bytes 6291464 | tf_op jit(solution)/shard_map/ppermute | solution.py:30
  510.0 46.9 %collective-permute-start.13 = (f32[32,64,256]{2,1,0:T(8,128)S(1)}, f32[32,64,256]{2,1,0:T(8,128)S(1)}, u32[]{:S(2)}, u32[]{:S(2)}) collective-permute-start(f32[32,64,256]{2,1,0:T(8,128)S(1)} %broadcast_select_fusion.3), channel_id=1, source_target_pairs={{16,0},{17,1},{18,2},{19,3},{20,4},{21,5},{22,6},{23,7},{24,8},{25... | collective-permute-start | bytes 6291464 | tf_op jit(solution)/shard_map/ppermute | solution.py:30
Sparse Core Ops, SparseCore 0:
  558.7 176.4 all-reduce.1
where the time goes:
time: 752 us; the launch traced here: 746 us
  waiting for transfers between devices  634 us (84%)
  starting transfers between devices  39.8 us (5%)
  matrix products  26.3 us (3%)
  other arithmetic  26.2 us (3%)
  between operations  15.1 us (2%)
    ppermute x10, waiting for transfers between devices, from_behind(): return lax.ppermute(block, axis, route)  448 us
    psum x1, waiting for transfers between devices, body(): summed = lax.psum(log_terms, 'view')  177 us
    ppermute x10, starting transfers between devices, from_behind(): return lax.ppermute(block, axis, route)  35.5 us
    dot_general x10, matrix products, matmul_high(): jnp.dot(left, right, precision=lax.Precision.HIGHEST, preferred_element_t...  26.3 us
  transfers between devices with their start and end apart: 15, of which 14 were waited for; matrix products, arithmetic and copies ran while one was open for 0% of the time, Pallas kernels for 0%

commit v1 on v0

--- a/solution.py
+++ b/solution.py
@@ -92,7 +92,7 @@
         arrived = from_behind(correction, "tile", stride)
         correction = jnp.where(tile_move // stride % 2 == 1, arrived, correction)
     log_terms = jnp.log(correction)
-    summed = lax.psum(log_terms, "view")
+    summed = jnp.sum(lax.all_gather(log_terms, "view"), axis=0)
     return estimate * jnp.exp(summed)
 
 

time: 752 us -> 848 us (1.13)
  waiting for transfers between devices: 634 us -> 720 us
  other arithmetic: 26.2 us -> 35.3 us
    all_gather x0 -> x1, waiting for transfers between devices: none -> 262 us  [body(): summed = jnp.sum(lax.all_gather(log_terms, 'view'), axis=0)]
    psum x1 -> x0, waiting for transfers between devices: 177 us -> none  [body(): summed = lax.psum(log_terms, 'view')]
    reduce_sum x0 -> x1, other arithmetic: none -> 9.08 us  [body(): summed = jnp.sum(lax.all_gather(log_terms, 'view'), axis=0)]
where the time goes in v1:
time: 848 us; the launch traced here: 841 us
  waiting for transfers between devices  720 us (85%)
  starting transfers between devices  40.2 us (5%)
  other arithmetic  35.3 us (4%)
  matrix products  26.3 us (3%)
  between operations  15.2 us (2%)
    ppermute x10, waiting for transfers between devices, from_behind(): return lax.ppermute(block, axis, route)  448 us
    all_gather x1, waiting for transfers between devices, body(): summed = jnp.sum(lax.all_gather(log_terms, 'view'), axis=0)  262 us
    ppermute x10, starting transfers between devices, from_behind(): return lax.ppermute(block, axis, route)  35.7 us
    dot_general x10, matrix products, matmul_high(): jnp.dot(left, right, precision=lax.Precision.HIGHEST, preferred_element_t...  26.3 us
  transfers between devices with their start and end apart: 15, of which 14 were waited for; matrix products, arithmetic and copies ran while one was open for 0% of the time, Pallas kernels for 0%

profile of v1, /device:TPU:32, one launch (start us, length us, event | category | flops | bytes accessed | tf_op | source)
XLA Modules:
  0.0 840.9 jit_solution(14301184715680245060)
XLA Ops:
  10.1 12.0 %collective-permute-done = bf16[32,64,256]{2,1,0:T(8,128)(2,1)S(1)} collective-permute-done((bf16[32,64,256]{2,1,0:T(8,128)(2,1)}, bf16[32,64,256]{2,1,0:T(8,128)(2,1)S(1)}, u32[]{:S(2)}, u32[]{:S(2)}) %collective-permute-start) | collective-permute-done | bytes 1048608 | tf_op jit(solution)/shard_map/ppermute | solution.py:30
  23.4 8.0 collective-permute-start.1
  31.4 17.2 %collective-permute-done.1 = bf16[32,64,256]{2,1,0:T(8,128)(2,1)} collective-permute-done((bf16[32,64,256]{2,1,0:T(8,128)(2,1)}, bf16[32,64,256]{2,1,0:T(8,128)(2,1)}, u32[]{:S(2)}, u32[]{:S(2)}) %collective-permute-start.1) | collective-permute-done | bytes 1048608 | tf_op jit(solution)/shard_map/ppermute | solution.py:30
  48.6 3.5 fusion.112
  52.1 9.3 %collective-permute-start.2 = (bf16[32,64,256]{2,1,0:T(8,128)(2,1)}, bf16[32,64,256]{2,1,0:T(8,128)(2,1)S(1)}, u32[]{:S(2)}, u32[]{:S(2)}) collective-permute-start(bf16[32,64,256]{2,1,0:T(8,128)(2,1)} %get-tuple-element.5), channel_id=1, source_target_pairs={{4,0},{5,1},{6,2},{7,3},{8,4},{9,5},{10,6},{11,7},{12,8},{13,9},{1... | collective-permute-start | bytes 3145736 | tf_op jit(solution)/shard_map/ppermute | solution.py:30
  61.4 41.3 %collective-permute-done.2 = bf16[32,64,256]{2,1,0:T(8,128)(2,1)S(1)} collective-permute-done((bf16[32,64,256]{2,1,0:T(8,128)(2,1)}, bf16[32,64,256]{2,1,0:T(8,128)(2,1)S(1)}, u32[]{:S(2)}, u32[]{:S(2)}) %collective-permute-start.2) | collective-permute-done | bytes 1048608 | tf_op jit(solution)/shard_map/ppermute | solution.py:30
  104.1 9.1 %collective-permute-start.3 = (bf16[32,64,256]{2,1,0:T(8,128)(2,1)}, bf16[32,64,256]{2,1,0:T(8,128)(2,1)}, u32[]{:S(2)}, u32[]{:S(2)}) collective-permute-start(bf16[32,64,256]{2,1,0:T(8,128)(2,1)} %fusion.23), channel_id=1, source_target_pairs={{8,0},{9,1},{10,2},{11,3},{12,4},{13,5},{14,6},{15,7},{16,8},{17,9... | collective-permute-start | bytes 3145736 | tf_op jit(solution)/shard_map/ppermute | solution.py:30
  113.2 45.5 %collective-permute-done.3 = bf16[32,64,256]{2,1,0:T(8,128)(2,1)} collective-permute-done((bf16[32,64,256]{2,1,0:T(8,128)(2,1)}, bf16[32,64,256]{2,1,0:T(8,128)(2,1)}, u32[]{:S(2)}, u32[]{:S(2)}) %collective-permute-start.3) | collective-permute-done | bytes 1048608 | tf_op jit(solution)/shard_map/ppermute | solution.py:30
  163.9 23.7 %collective-permute-done.4 = bf16[32,64,256]{2,1,0:T(8,128)(2,1)} collective-permute-done((bf16[32,64,256]{2,1,0:T(8,128)(2,1)}, bf16[32,64,256]{2,1,0:T(8,128)(2,1)}, u32[]{:S(2)}, u32[]{:S(2)}) %collective-permute-start.4) | collective-permute-done | bytes 1048608 | tf_op jit(solution)/shard_map/ppermute | solution.py:30
  202.1 2.9 fusion.35
  207.9 3.0 fusion.8
  210.9 3.3 convert_divide_fusion
  219.9 3.0 fusion
  222.9 3.2 subtract_multiply_fusion
  230.5 6.4 collective-permute-done.7
  239.6 25.3 %collective-permute-done.9 = f32[32,64,256]{2,1,0:T(8,128)S(1)} collective-permute-done((f32[32,64,256]{2,1,0:T(8,128)S(1)}, f32[32,64,256]{2,1,0:T(8,128)S(1)}, u32[]{:S(2)}, u32[]{:S(2)}) %collective-permute-start.9) | collective-permute-done | bytes 2097184 | tf_op jit(solution)/shard_map/ppermute | solution.py:30
  266.0 45.6 %collective-permute-done.10 = f32[32,64,256]{2,1,0:T(8,128)S(1)} collective-permute-done((f32[32,64,256]{2,1,0:T(8,128)S(1)}, f32[32,64,256]{2,1,0:T(8,128)S(1)}, u32[]{:S(2)}, u32[]{:S(2)}) %collective-permute-start.10) | collective-permute-done | bytes 2097184 | tf_op jit(solution)/shard_map/ppermute | solution.py:30
  312.0 5.0 collective-permute-start.11
  317.0 94.2 %collective-permute-done.11 = f32[32,64,256]{2,1,0:T(8,128)S(1)} collective-permute-done((f32[32,64,256]{2,1,0:T(8,128)S(1)}, f32[32,64,256]{2,1,0:T(8,128)S(1)}, u32[]{:S(2)}, u32[]{:S(2)}) %collective-permute-start.11) | collective-permute-done | bytes 2097184 | tf_op jit(solution)/shard_map/ppermute | solution.py:30
  411.7 97.9 %collective-permute-done.12 = f32[32,64,256]{2,1,0:T(8,128)S(1)} collective-permute-done((f32[32,64,256]{2,1,0:T(8,128)S(1)}, f32[32,64,256]{2,1,0:T(8,128)S(1)}, u32[]{:S(2)}, u32[]{:S(2)}) %collective-permute-start.12) | collective-permute-done | bytes 2097184 | tf_op jit(solution)/shard_map/ppermute | solution.py:30
  511.6 45.6 %collective-permute-done.13 = f32[32,64,256]{2,1,0:T(8,128)S(1)} collective-permute-done((f32[32,64,256]{2,1,0:T(8,128)S(1)}, f32[32,64,256]{2,1,0:T(8,128)S(1)}, u32[]{:S(2)}, u32[]{:S(2)}) %collective-permute-start.13) | collective-permute-done | bytes 2097184 | tf_op jit(solution)/shard_map/ppermute | solution.py:30
  558.9 262.4 %all-gather.3.cloned.1.call-done = f32[256,64,256]{2,1,0:T(8,128)} async-done(((f32[32,64,256]{2,1,0:T(8,128)}), f32[256,64,256]{2,1,0:T(8,128)}) %all-gather.3.cloned.1.call-update) | async-done | bytes 16777232 | tf_op jit(solution)/shard_map/all_gather | solution.py:95
  821.3 9.1 %reduce_sum.19 = f32[32,64,256]{2,1,0:T(8,128)} reduce(f32[8,32,64,256]{3,2,1,0:T(8,128)} %bitcast.44, f32[]{:T(128)} %constant.157.clone.1), dimensions={0}, to_apply=%region_1.2 | reduce | flops 3670016 | bytes 18874372 | tf_op jit(solution)/shard_map/reduce_sum | solution.py:95
  830.4 3.4 exponential_multiply_fusion
  (48 shorter events, 45.7 us)
Async XLA Ops:
  6.5 15.5 %copy-start = (f32[32,64,256]{2,1,0:T(8,128)S(1)}, f32[32,64,256]{2,1,0:T(8,128)}, u32[]{:S(2)}) copy-start(f32[32,64,256]{2,1,0:T(8,128)} %param.5) | copy-start | bytes 6291460
  6.5 814.8 %all-gather.3.cloned.1.call-start = ((), (), s32[]{:S(2)}) async-start(), calls=%async_computation | async-start | bytes 18874368 | tf_op jit(solution)/shard_map/all_gather | solution.py:95
  9.4 12.6 %collective-permute-start = (bf16[32,64,256]{2,1,0:T(8,128)(2,1)}, bf16[32,64,256]{2,1,0:T(8,128)(2,1)S(1)}, u32[]{:S(2)}, u32[]{:S(2)}) collective-permute-start(bf16[32,64,256]{2,1,0:T(8,128)(2,1)} %convert_element_type.66), channel_id=1, source_target_pairs={{1,0},{2,1},{3,2},{4,3},{5,4},{6,5},{7,6},{8,7},{9,8},{10,9},{11,1... | collective-permute-start | bytes 3145736 | tf_op jit(solution)/shard_map/ppermute | solution.py:30
  23.4 25.3 %collective-permute-start.1 = (bf16[32,64,256]{2,1,0:T(8,128)(2,1)}, bf16[32,64,256]{2,1,0:T(8,128)(2,1)}, u32[]{:S(2)}, u32[]{:S(2)}) collective-permute-start(bf16[32,64,256]{2,1,0:T(8,128)(2,1)} %fusion.22), channel_id=1, source_target_pairs={{2,0},{3,1},{4,2},{5,3},{6,4},{7,5},{8,6},{9,7},{10,8},{11,9},{12,... | collective-permute-start | bytes 3145736 | tf_op jit(solution)/shard_map/ppermute | solution.py:30
  52.1 50.7 %collective-permute-start.2 = (bf16[32,64,256]{2,1,0:T(8,128)(2,1)}, bf16[32,64,256]{2,1,0:T(8,128)(2,1)S(1)}, u32[]{:S(2)}, u32[]{:S(2)}) collective-permute-start(bf16[32,64,256]{2,1,0:T(8,128)(2,1)} %get-tuple-element.5), channel_id=1, source_target_pairs={{4,0},{5,1},{6,2},{7,3},{8,4},{9,5},{10,6},{11,7},{12,8},{13,9},{1... | collective-permute-start | bytes 3145736 | tf_op jit(solution)/shard_map/ppermute | solution.py:30
  104.1 54.6 %collective-permute-start.3 = (bf16[32,64,256]{2,1,0:T(8,128)(2,1)}, bf16[32,64,256]{2,1,0:T(8,128)(2,1)}, u32[]{:S(2)}, u32[]{:S(2)}) collective-permute-start(bf16[32,64,256]{2,1,0:T(8,128)(2,1)} %fusion.23), channel_id=1, source_target_pairs={{8,0},{9,1},{10,2},{11,3},{12,4},{13,5},{14,6},{15,7},{16,8},{17,9... | collective-permute-start | bytes 3145736 | tf_op jit(solution)/shard_map/ppermute | solution.py:30
  113.2 50.1 %copy-start.3 = (f32[1,256]{1,0:T(1,128)S(1)}, f32[1,256]{1,0:T(1,128)}, u32[]{:S(2)}) copy-start(f32[1,256]{1,0:T(1,128)} %param.7) | copy-start | bytes 3076
  161.4 26.2 %collective-permute-start.4 = (bf16[32,64,256]{2,1,0:T(8,128)(2,1)}, bf16[32,64,256]{2,1,0:T(8,128)(2,1)}, u32[]{:S(2)}, u32[]{:S(2)}) collective-permute-start(bf16[32,64,256]{2,1,0:T(8,128)(2,1)} %fusion.34), channel_id=1, source_target_pairs={{16,0},{17,1},{18,2},{19,3},{20,4},{21,5},{22,6},{23,7},{24,8},{25... | collective-permute-start | bytes 3145736 | tf_op jit(solution)/shard_map/ppermute | solution.py:30
  189.8 1.3 copy-start.2
  191.9 8.1 collective-permute-start.5
  191.9 8.2 collective-permute-start.6
  207.9 3.0 copy-start.4
  226.1 1.3 copy-start.1
  228.3 8.6 %collective-permute-start.7 = (f32[7,64,256]{2,1,0:T(8,128)}, f32[7,64,256]{2,1,0:T(8,128)S(1)}, u32[]{:S(2)}, u32[]{:S(2)}) collective-permute-start(f32[7,64,256]{2,1,0:T(8,128)} %get-tuple-element.7), channel_id=1, source_target_pairs={{0,1},{1,2},{2,3},{3,4},{4,5},{5,6},{6,7},{7,8},{8,9},{9,10},{10,1... | collective-permute-start | bytes 1376264 | tf_op jit(solution)/shard_map/ppermute | solution.py:18
  229.2 7.6 collective-permute-start.8
  239.3 25.6 %collective-permute-start.9 = (f32[32,64,256]{2,1,0:T(8,128)S(1)}, f32[32,64,256]{2,1,0:T(8,128)S(1)}, u32[]{:S(2)}, u32[]{:S(2)}) collective-permute-start(f32[32,64,256]{2,1,0:T(8,128)S(1)} %multiply_add_fusion), channel_id=1, source_target_pairs={{31,0},{0,1},{1,2},{2,3},{3,4},{4,5},{5,6},{6,7},{7,8},{8,9},{9,10... | collective-permute-start | bytes 6291464 | tf_op jit(solution)/shard_map/ppermute | solution.py:30
  265.7 46.0 %collective-permute-start.10 = (f32[32,64,256]{2,1,0:T(8,128)S(1)}, f32[32,64,256]{2,1,0:T(8,128)S(1)}, u32[]{:S(2)}, u32[]{:S(2)}) collective-permute-start(f32[32,64,256]{2,1,0:T(8,128)S(1)} %broadcast_select_fusion), channel_id=1, source_target_pairs={{30,0},{31,1},{0,2},{1,3},{2,4},{3,5},{4,6},{5,7},{6,8},{7,9},{8,1... | collective-permute-start | bytes 6291464 | tf_op jit(solution)/shard_map/ppermute | solution.py:30
  312.0 99.3 %collective-permute-start.11 = (f32[32,64,256]{2,1,0:T(8,128)S(1)}, f32[32,64,256]{2,1,0:T(8,128)S(1)}, u32[]{:S(2)}, u32[]{:S(2)}) collective-permute-start(f32[32,64,256]{2,1,0:T(8,128)S(1)} %broadcast_select_fusion.1), channel_id=1, source_target_pairs={{28,0},{29,1},{30,2},{31,3},{0,4},{1,5},{2,6},{3,7},{4,8},{5,9},{6... | collective-permute-start | bytes 6291464 | tf_op jit(solution)/shard_map/ppermute | solution.py:30
  411.6 98.0 %collective-permute-start.12 = (f32[32,64,256]{2,1,0:T(8,128)S(1)}, f32[32,64,256]{2,1,0:T(8,128)S(1)}, u32[]{:S(2)}, u32[]{:S(2)}) collective-permute-start(f32[32,64,256]{2,1,0:T(8,128)S(1)} %broadcast_select_fusion.2), channel_id=1, source_target_pairs={{24,0},{25,1},{26,2},{27,3},{28,4},{29,5},{30,6},{31,7},{0,8},{1,9... | collective-permute-start | bytes 6291464 | tf_op jit(solution)/shard_map/ppermute | solution.py:30
  510.1 47.2 %collective-permute-start.13 = (f32[32,64,256]{2,1,0:T(8,128)S(1)}, f32[32,64,256]{2,1,0:T(8,128)S(1)}, u32[]{:S(2)}, u32[]{:S(2)}) collective-permute-start(f32[32,64,256]{2,1,0:T(8,128)S(1)} %broadcast_select_fusion.3), channel_id=1, source_target_pairs={{16,0},{17,1},{18,2},{19,3},{20,4},{21,5},{22,6},{23,7},{24,8},{25... | collective-permute-start | bytes 6291464 | tf_op jit(solution)/shard_map/ppermute | solution.py:30
Sparse Core Ops, SparseCore 0:
  559.0 262.2 all-gather.2
